TPU v7x, 32 devices: a whole 2x2x4 slice. The times are simulated.
32 devices in a mesh: kv: 2 (over x), seq: 16 (over z, y, core).
Axes of the slice: x: 2, y: 2, z: 4, core: 2. Of those that a mesh axis runs over, the one named last changes fastest.
Arguments:
- hidden: bfloat16 [1024, 2048], P('seq', 'kv'), may hold values from -1.5 to 1.5
- in_gain: float32 [2048], replicated, may hold values from 0.5 to 1.5
- w_query: bfloat16 [2048, 2048], P(None, 'kv'), may hold values from -0.125 to 0.125
- key_projection_weight: bfloat16 [2048, 1024], P(None, 'kv'), may hold values from -0.125 to 0.125
- value_projection_weight: bfloat16 [2048, 1024], P(None, 'kv'), may hold values from -0.125 to 0.125
- w_gate: bfloat16 [2048, 16], P(None, 'kv'), may hold values from -0.125 to 0.125
- w_out: bfloat16 [2048, 2048], P('kv'), may hold values from -0.125 to 0.125
- q_gain: float32 [128], replicated, may hold values from 0.1 to 1.9
- k_gain: float32 [128], replicated, may hold values from 0.1 to 1.9
- cache_keys: bfloat16 [32768, 8, 128], P('seq', 'kv'), may hold values from -160 to 160
- pooled_cache_values: bfloat16 [32768, 8, 128], P('seq', 'kv'), may hold values from -6 to 6
- prefix_len: int32 [4], replicated, may hold values from 1024 to 8192, as said below
- own_len: int32 [32], replicated, may hold values from 256 to 2048, as said below
- request_group: int32 [32], replicated, may hold values from 0 to 3, as said below
- parents: int32 [32, 32], P('seq'), may hold values from 0 to 30, as said below
- accepted_leaf: int32 [32], P('seq'), may hold values from 0 to 31
Outputs:
- layer_out: bfloat16 [1024, 2048], P('seq', 'kv')
- accepted_keys: bfloat16 [32, 32, 1024], P('seq', None, 'kv')
- accepted_values: bfloat16 [32, 32, 1024], P('seq', None, 'kv')
Inputs may be any that keep to these rules, and one draw needn't show every extreme that they name: parents[r, 0] is 0 and node 0 is the root; for i >= 1, parents[r, i] < i. `prefix_len`: the lengths sum to 32768 // 2; one is exactly 8192 and one exactly 1024. `own_len`: the lengths sum to 32768 // 2; one is exactly 2048 and one exactly 256. `request_group`: every group holds exactly 8 requests.
All inputs are finite; a program needn't handle non-finite values.
Results may differ from a plain program's by a relative error of at most 0.017.
The roundings to bfloat16 on the way count: a program that leaves them out, or rounds other values in their place, can miss the bound.
Values may be sent and summed in bfloat16 or wider, within the bound.
A program may use at most 128 MiB of HBM per device.

v0:
```python
import math
import jax
import jax.numpy as jnp
from jax import lax
from jax.sharding import PartitionSpec as P

EPSILON = 1e-06
ROPE_BASE = 1000000.0
NEGATIVE = -1e30


def rms_scale(values, scales):
    mean_square = jnp.mean(values * values, axis=-1, keepdims=True)
    return values * lax.rsqrt(mean_square + EPSILON) * scales


def rotate_pairs(values, positions):
    half_width = values.shape[-1] // 2
    freqs = jnp.exp(
        jnp.arange(half_width, dtype=jnp.float32) * (-2.0 * math.log(ROPE_BASE) / values.shape[-1])
    )
    angles = positions[:, None] * freqs[None, :]
    cosine = jnp.concatenate([jnp.cos(angles), jnp.cos(angles)], axis=-1)[:, None, :]
    sine = jnp.concatenate([jnp.sin(angles), jnp.sin(angles)], axis=-1)[:, None, :]
    turned = jnp.concatenate([-values[..., half_width:], values[..., :half_width]], axis=-1)
    return values * cosine + turned * sine


def tree_paths(parents):
    width = parents.shape[-1]
    nodes = jnp.arange(width, dtype=jnp.int32)
    linked = (parents[:, :, None] == nodes[None, None, :]).astype(jnp.float32)
    identity_mat = jnp.eye(width, dtype=jnp.float32)
    reach = jnp.minimum(identity_mat[None] + linked * (1.0 - identity_mat[None]), 1.0)
    for squaring in range(max(1, (width - 1).bit_length())):
        reach = jnp.minimum(
            jnp.einsum("mij,mjk->mik", reach, reach, precision=lax.Precision.HIGHEST), 1.0
        )
    depth_f = jnp.sum(reach, axis=-1) - 1.0
    return (reach, depth_f)


def accepted_rows(reach, depth_f, leaves, tree_rows):
    width = reach.shape[-1]
    nodes = jnp.arange(width, dtype=jnp.int32)
    leaf_pick = (leaves[:, None] == nodes[None, :]).astype(jnp.float32)
    on_path = jnp.einsum("mi,mij->mj", leaf_pick, reach, precision=lax.Precision.HIGHEST)
    levels = (depth_f[:, None, :] == nodes.astype(jnp.float32)[None, :, None]).astype(jnp.float32)
    select = levels * on_path[:, None, :]
    return jnp.einsum(
        "mdj,mjc->mdc", select, tree_rows.astype(jnp.float32), precision=lax.Precision.HIGHEST
    ).astype(jnp.bfloat16)


def body(
    hidden,
    in_gain,
    w_query,
    key_projection_weight,
    value_projection_weight,
    w_gate,
    w_out,
    q_gain,
    k_gain,
    cache_keys,
    pooled_cache_values,
    prefix_len,
    own_len,
    request_group,
    parents,
    accepted_leaf,
):
    local_req, tree = parents.shape
    groups = prefix_len.shape[0]
    requests = own_len.shape[0]
    head_width = q_gain.shape[0]
    local_heads = w_gate.shape[1]
    local_kv = key_projection_weight.shape[1] // head_width
    per_kv = local_heads // local_kv
    local_tok = hidden.shape[0]
    pool_dev = cache_keys.shape[0]
    seq_index = lax.axis_index("seq")
    score_scale = 1.0 / math.sqrt(head_width)
    full_rows = lax.all_gather(hidden, "kv", axis=1, tiled=True)
    normed = rms_scale(full_rows.astype(jnp.float32), in_gain).astype(jnp.bfloat16)
    reach, depth_f = tree_paths(parents)
    all_reqs = jnp.arange(requests, dtype=jnp.int32)
    my_reqs = seq_index * local_req + jnp.arange(local_req, dtype=jnp.int32)
    my_pick = (my_reqs[:, None] == all_reqs[None, :]).astype(jnp.int32)
    my_group = jnp.sum(my_pick * request_group[None, :], axis=1)
    group_ids = jnp.arange(groups, dtype=jnp.int32)
    group_pick = (my_group[:, None] == group_ids[None, :]).astype(jnp.int32)
    context = jnp.sum(group_pick * prefix_len[None, :], axis=1) + jnp.sum(
        my_pick * own_len[None, :], axis=1
    )
    positions = (context[:, None].astype(jnp.float32) + depth_f).reshape(-1)
    query = jnp.dot(normed, w_query, preferred_element_type=jnp.float32).reshape(
        local_tok, local_heads, head_width
    )
    query = rotate_pairs(rms_scale(query, q_gain), positions).astype(jnp.bfloat16)
    key_new = jnp.dot(normed, key_projection_weight, preferred_element_type=jnp.float32).reshape(
        local_tok, local_kv, head_width
    )
    key_new = rotate_pairs(rms_scale(key_new, k_gain), positions).astype(jnp.bfloat16)
    value_new = (
        jnp.dot(normed, value_projection_weight, preferred_element_type=jnp.float32)
        .astype(jnp.bfloat16)
        .reshape(local_tok, local_kv, head_width)
    )
    gate_logit = jnp.dot(normed, w_gate, preferred_element_type=jnp.float32)
    tree_query = query.reshape(local_req, tree, local_kv, per_kv, head_width)
    tree_keys = key_new.reshape(local_req, tree, local_kv, head_width)
    tree_values = value_new.reshape(local_req, tree, local_kv, head_width)
    tree_scores = (
        jnp.einsum("atkgd,askd->atkgs", tree_query, tree_keys, preferred_element_type=jnp.float32)
        * score_scale
    )
    tree_seen = (reach > 0.5)[:, :, None, None, :]
    tree_scores = jnp.where(tree_seen, tree_scores, NEGATIVE)
    tree_max = jnp.max(tree_scores, axis=-1)
    tree_weights = jnp.where(tree_seen, jnp.exp(tree_scores - tree_max[..., None]), 0.0)
    tree_sum = jnp.sum(tree_weights, axis=-1).reshape(local_tok, local_heads)
    tree_num = jnp.einsum(
        "atkgs,askd->atkgd",
        tree_weights.astype(jnp.bfloat16),
        tree_values,
        preferred_element_type=jnp.float32,
    ).reshape(local_tok, local_heads, head_width)
    tree_max = tree_max.reshape(local_tok, local_heads)
    lengths_all = jnp.concatenate([prefix_len, own_len])
    starts = jnp.cumsum(lengths_all) - lengths_all
    slot_ids = seq_index * pool_dev + jnp.arange(pool_dev, dtype=jnp.int32)
    slot_segment = jnp.sum((starts[None, :] <= slot_ids[:, None]).astype(jnp.int32), axis=1) - 1
    block_len = min(512, pool_dev)
    block_count = pool_dev // block_len
    key_blocks = cache_keys.reshape(block_count, block_len, local_kv, head_width)
    value_blocks = pooled_cache_values.reshape(block_count, block_len, local_kv, head_width)
    segment_blocks = slot_segment.reshape(block_count, block_len)
    query_flat = query.reshape(local_tok, local_heads * head_width)
    query_piece = lax.all_gather(query_flat, "seq", axis=0, tiled=True)
    row_ids = jnp.arange(query_piece.shape[0], dtype=jnp.int32)
    owners = row_ids // tree
    count = query_piece.shape[0]
    grouped = query_piece.reshape(count, local_kv, per_kv, head_width)
    owner_pick = (owners[:, None] == all_reqs[None, :]).astype(jnp.int32)
    known = owners >= 0
    prefix_segment = jnp.where(known, jnp.sum(owner_pick * request_group[None, :], axis=1), -5)
    own_segment = jnp.where(known, owners + groups, -5)

    def visit(carry, block):
        run_max, run_sum, run_num = carry
        keys_block, values_block, segment_block = block
        scores = (
            jnp.einsum("nkgd,pkd->nkgp", grouped, keys_block, preferred_element_type=jnp.float32)
            * score_scale
        )
        visible = (segment_block[None, :] == prefix_segment[:, None]) | (
            segment_block[None, :] == own_segment[:, None]
        )
        visible = visible[:, None, None, :]
        scores = jnp.where(visible, scores, NEGATIVE)
        new_max = jnp.maximum(run_max, jnp.max(scores, axis=-1))
        weights = jnp.where(visible, jnp.exp(scores - new_max[..., None]), 0.0)
        factor = jnp.exp(run_max - new_max)
        run_sum = run_sum * factor + jnp.sum(weights, axis=-1)
        run_num = run_num * factor[..., None] + jnp.einsum(
            "nkgp,pkd->nkgd",
            weights.astype(jnp.bfloat16),
            values_block,
            preferred_element_type=jnp.float32,
        )
        return ((new_max, run_sum, run_num), None)

    start_state = (
        jnp.full((count, local_kv, per_kv), NEGATIVE, jnp.float32),
        jnp.zeros((count, local_kv, per_kv), jnp.float32),
        jnp.zeros((count, local_kv, per_kv, head_width), jnp.float32),
    )
    final_state, unused = lax.scan(visit, start_state, (key_blocks, value_blocks, segment_blocks))
    run_max, run_sum, run_num = final_state
    part_max = run_max.reshape(count, local_heads)
    part_sum = run_sum.reshape(count, local_heads)
    part_num = run_num.reshape(count, local_heads * head_width)
    all_rows = part_max.shape[0]
    cache_max = lax.pmax(part_max.astype(jnp.bfloat16), "seq").astype(part_max.dtype)
    factor = jnp.exp(part_max - cache_max)
    scaled_num = (part_num.reshape(all_rows, local_heads, head_width) * factor[..., None]).reshape(
        all_rows, local_heads * head_width
    )
    summed_num, summed_sum = (
        lax.psum_scatter(
            scaled_num.astype(jnp.bfloat16), "seq", scatter_dimension=0, tiled=True
        ).astype(jnp.float32),
        lax.psum_scatter(
            (part_sum * factor).astype(jnp.bfloat16), "seq", scatter_dimension=0, tiled=True
        ).astype(jnp.float32),
    )
    own_max = lax.dynamic_slice_in_dim(cache_max, seq_index * local_tok, local_tok, 0)
    final_max = jnp.maximum(own_max, tree_max)
    cache_factor = jnp.exp(own_max - final_max)
    tree_factor = jnp.exp(tree_max - final_max)
    weight_sum = summed_sum * cache_factor + tree_sum * tree_factor
    mixed = (
        summed_num.reshape(local_tok, local_heads, head_width) * cache_factor[..., None]
        + tree_num * tree_factor[..., None]
    )
    mixed = mixed / weight_sum[..., None]
    attended = (
        (mixed * jax.nn.sigmoid(gate_logit)[..., None])
        .astype(jnp.bfloat16)
        .reshape(local_tok, local_heads * head_width)
    )
    projected = jnp.dot(attended, w_out, preferred_element_type=jnp.float32)
    layer_part = lax.psum_scatter(
        projected.astype(jnp.bfloat16), "kv", scatter_dimension=1, tiled=True
    ).astype(jnp.float32)
    layer_out = (layer_part + hidden.astype(jnp.float32)).astype(jnp.bfloat16)
    tree_rows = jnp.concatenate(
        [
            key_new.reshape(local_req, tree, local_kv * head_width),
            value_new.reshape(local_req, tree, local_kv * head_width),
        ],
        axis=-1,
    )
    picked = accepted_rows(reach, depth_f, accepted_leaf, tree_rows)
    accepted_keys = picked[:, :, : local_kv * head_width]
    accepted_values = picked[:, :, local_kv * head_width :]
    return (layer_out, accepted_keys, accepted_values)


def solution(mesh):
    in_specs = (
        P("seq", "kv"),
        P(),
        P(None, "kv"),
        P(None, "kv"),
        P(None, "kv"),
        P(None, "kv"),
        P("kv", None),
        P(),
        P(),
        P("seq", "kv", None),
        P("seq", "kv", None),
        P(),
        P(),
        P(),
        P("seq", None),
        P("seq"),
    )
    out_specs = (P("seq", "kv"), P("seq", None, "kv"), P("seq", None, "kv"))
    return jax.shard_map(body, mesh=mesh, in_specs=in_specs, out_specs=out_specs, check_vma=False)
```

profile of v0, /device:TPU:0, one launch (start us, length us, event | category | flops | bytes accessed | tf_op | source)
XLA Modules:
  0.0 365.4 jit_solution(637547949621892404)
XLA Ops:
  7.3 0.8 broadcast_bitcast_fusion
  8.1 7.4 %all_gather.6 = bf16[64,2048]{1,0:T(8,128)(2,1)S(1)} all-gather(bf16[64,1024]{1,0:T(8,128)(2,1)} %param.18), channel_id=1, replica_groups=mesh['kv'=2,'seq'=16] {'kv'}, dimensions={1}, use_global_device_ids=true | all-gather | bytes 393216 | tf_op jit(solution)/shard_map/all_gather | solution.py:84
  15.6 3.1 fusion.96
  22.7 0.8 fusion.35
  25.8 0.9 fusion.28
  26.7 39.9 %all-gather.2.cloned.1.call-done = bf16[1024,1024]{1,0:T(8,128)(2,1)} async-done(((bf16[64,1024]{1,0:T(8,128)(2,1)}), bf16[1024,1024]{1,0:T(8,128)(2,1)}) %all-gather.2.cloned.1.call-update) | async-done | bytes 2097168 | tf_op jit(solution)/shard_map/all_gather | solution.py:140
  66.6 4.5 %reshape.343 = bf16[1024,4,2,128]{3,2,1,0:T(2,128)(2,1)} reshape(bf16[1024,1024]{1,0:T(8,128)(2,1)} %all-gather.2.cloned.1.call-done) | data formatting | bytes 4194304 | tf_op jit(solution)/shard_map/reshape | solution.py:144
  71.1 3.2 copy.172
  74.3 84.1 %while.15 = (s32[]{:T(128)}, f32[1024,4,2]{0,2,1:T(2,128)S(1)}, f32[1024,4,2]{0,2,1:T(2,128)S(1)}, f32[1024,4,2,128]{0,3,2,1:T(8,128)}, s32[4,512]{1,0:T(4,128)S...) while((s32[]{:T(128)}, f32[1024,4,2]{0,2,1:T(2,128)S(1)}, ...), condition=%wide.region_12.13_spmd.clone, body=%wide.region_9.12_spmd.clone.sunk | while | flops 2206780416 | bytes 69748896 | solution.py:179
  74.7 2.4 constant_dynamic-slice_fusion.6
  77.1 1.1 copy.285
  78.2 4.6 %fusion.137 = (f32[1024,4,2]{0,2,1:T(2,128)S(1)}, f32[4,512,1024,2]{2,1,3,0:T(8,128)S(1)}) fusion(pred[1024,512]{0,1:T(8,128)(4,1)S(1)} %compare_or_fusion.2, bf16[1024,4,2,128]{3,0,2,1:T(8,128)(2,1)} %get-tuple-element.291, bf16[1,512,4,128]{3,2,1,0:T(4,128)(2,1)} %get-tuple-element.256), kind=kOutput, calls=%fused_computation.3.clone.1 | convolution fusion | flops 1086316544 | bytes 19955712 | tf_op jit(solution)/shard_map/while/body/eval_jaxpr/nkgd,pkd->nkgp/dot_general | solution.py:154
  82.8 4.1 %fusion.139 = f32[1024,4,2]{0,2,1:T(2,128)S(1)} fusion(f32[4,512,1024,2]{2,1,3,0:T(8,128)S(1)} %get-tuple-element.258, f32[1024,4,2]{0,2,1:T(2,128)S(1)} %fusion.138, pred[1024,512]{0,1:T(8,128)(4,1)S(1)} %compare_or_fusion.2), kind=kLoop, calls=%fused_computation.5.clone.1 | loop fusion | flops 20963328 | bytes 17367040 | tf_op jit(solution)/shard_map/while/body/eval_jaxpr/reduce_sum | solution.py:165
  87.0 7.1 %bitcast_add_fusion.2 = f32[1024,4,2,128]{0,3,2,1:T(8,128)} fusion(f32[1024,4,2,128]{0,3,2,1:T(8,128)} %get-tuple-element.276, f32[4,512,1024,2]{2,1,3,0:T(8,128)S(1)} %get-tuple-element.258, f32[1024,4,2]{0,2,1:T(2,128)S(1)} %fusion.138, pred[1024,512]{0,1:T(8,128)(4,1)S(1)} %compare_or_fusion.2, f32[1024,4,2]{0,2,1:T(2,128)S(1)} %get-tuple-element.260, ...), kind=kOutput, calls=%fused_computation.8.clone.1 | convolution fusion | flops 1097859072 | bytes 26279936 | tf_op jit(solution)/shard_map/while/body/eval_jaxpr/nkgp,pkd->nkgd/dot_general | solution.py:166
  94.6 2.4 constant_dynamic-slice_fusion.6
  96.9 1.1 copy.285
  98.1 4.6 %fusion.137 = (f32[1024,4,2]{0,2,1:T(2,128)S(1)}, f32[4,512,1024,2]{2,1,3,0:T(8,128)S(1)}) fusion(pred[1024,512]{0,1:T(8,128)(4,1)S(1)} %compare_or_fusion.2, bf16[1024,4,2,128]{3,0,2,1:T(8,128)(2,1)} %get-tuple-element.291, bf16[1,512,4,128]{3,2,1,0:T(4,128)(2,1)} %get-tuple-element.256), kind=kOutput, calls=%fused_computation.3.clone.1 | convolution fusion | flops 1086316544 | bytes 19955712 | tf_op jit(solution)/shard_map/while/body/eval_jaxpr/nkgd,pkd->nkgp/dot_general | solution.py:154
  102.7 4.1 %fusion.139 = f32[1024,4,2]{0,2,1:T(2,128)S(1)} fusion(f32[4,512,1024,2]{2,1,3,0:T(8,128)S(1)} %get-tuple-element.258, f32[1024,4,2]{0,2,1:T(2,128)S(1)} %fusion.138, pred[1024,512]{0,1:T(8,128)(4,1)S(1)} %compare_or_fusion.2), kind=kLoop, calls=%fused_computation.5.clone.1 | loop fusion | flops 20963328 | bytes 17367040 | tf_op jit(solution)/shard_map/while/body/eval_jaxpr/reduce_sum | solution.py:165
  106.9 8.7 %bitcast_add_fusion.2 = f32[1024,4,2,128]{0,3,2,1:T(8,128)} fusion(f32[1024,4,2,128]{0,3,2,1:T(8,128)} %get-tuple-element.276, f32[4,512,1024,2]{2,1,3,0:T(8,128)S(1)} %get-tuple-element.258, f32[1024,4,2]{0,2,1:T(2,128)S(1)} %fusion.138, pred[1024,512]{0,1:T(8,128)(4,1)S(1)} %compare_or_fusion.2, f32[1024,4,2]{0,2,1:T(2,128)S(1)} %get-tuple-element.260, ...), kind=kOutput, calls=%fused_computation.8.clone.1 | convolution fusion | flops 1097859072 | bytes 26279936 | tf_op jit(solution)/shard_map/while/body/eval_jaxpr/nkgp,pkd->nkgd/dot_general | solution.py:166
  116.0 2.4 constant_dynamic-slice_fusion.6
  118.4 1.1 copy.285
  119.5 4.6 %fusion.137 = (f32[1024,4,2]{0,2,1:T(2,128)S(1)}, f32[4,512,1024,2]{2,1,3,0:T(8,128)S(1)}) fusion(pred[1024,512]{0,1:T(8,128)(4,1)S(1)} %compare_or_fusion.2, bf16[1024,4,2,128]{3,0,2,1:T(8,128)(2,1)} %get-tuple-element.291, bf16[1,512,4,128]{3,2,1,0:T(4,128)(2,1)} %get-tuple-element.256), kind=kOutput, calls=%fused_computation.3.clone.1 | convolution fusion | flops 1086316544 | bytes 19955712 | tf_op jit(solution)/shard_map/while/body/eval_jaxpr/nkgd,pkd->nkgp/dot_general | solution.py:154
  124.1 4.1 %fusion.139 = f32[1024,4,2]{0,2,1:T(2,128)S(1)} fusion(f32[4,512,1024,2]{2,1,3,0:T(8,128)S(1)} %get-tuple-element.258, f32[1024,4,2]{0,2,1:T(2,128)S(1)} %fusion.138, pred[1024,512]{0,1:T(8,128)(4,1)S(1)} %compare_or_fusion.2), kind=kLoop, calls=%fused_computation.5.clone.1 | loop fusion | flops 20963328 | bytes 17367040 | tf_op jit(solution)/shard_map/while/body/eval_jaxpr/reduce_sum | solution.py:165
  128.3 8.7 %bitcast_add_fusion.2 = f32[1024,4,2,128]{0,3,2,1:T(8,128)} fusion(f32[1024,4,2,128]{0,3,2,1:T(8,128)} %get-tuple-element.276, f32[4,512,1024,2]{2,1,3,0:T(8,128)S(1)} %get-tuple-element.258, f32[1024,4,2]{0,2,1:T(2,128)S(1)} %fusion.138, pred[1024,512]{0,1:T(8,128)(4,1)S(1)} %compare_or_fusion.2, f32[1024,4,2]{0,2,1:T(2,128)S(1)} %get-tuple-element.260, ...), kind=kOutput, calls=%fused_computation.8.clone.1 | convolution fusion | flops 1097859072 | bytes 26279936 | tf_op jit(solution)/shard_map/while/body/eval_jaxpr/nkgp,pkd->nkgd/dot_general | solution.py:166
  137.4 2.4 constant_dynamic-slice_fusion.6
  139.8 1.1 copy.285
  140.9 4.6 %fusion.137 = (f32[1024,4,2]{0,2,1:T(2,128)S(1)}, f32[4,512,1024,2]{2,1,3,0:T(8,128)S(1)}) fusion(pred[1024,512]{0,1:T(8,128)(4,1)S(1)} %compare_or_fusion.2, bf16[1024,4,2,128]{3,0,2,1:T(8,128)(2,1)} %get-tuple-element.291, bf16[1,512,4,128]{3,2,1,0:T(4,128)(2,1)} %get-tuple-element.256), kind=kOutput, calls=%fused_computation.3.clone.1 | convolution fusion | flops 1086316544 | bytes 19955712 | tf_op jit(solution)/shard_map/while/body/eval_jaxpr/nkgd,pkd->nkgp/dot_general | solution.py:154
  145.5 4.1 %fusion.139 = f32[1024,4,2]{0,2,1:T(2,128)S(1)} fusion(f32[4,512,1024,2]{2,1,3,0:T(8,128)S(1)} %get-tuple-element.258, f32[1024,4,2]{0,2,1:T(2,128)S(1)} %fusion.138, pred[1024,512]{0,1:T(8,128)(4,1)S(1)} %compare_or_fusion.2), kind=kLoop, calls=%fused_computation.5.clone.1 | loop fusion | flops 20963328 | bytes 17367040 | tf_op jit(solution)/shard_map/while/body/eval_jaxpr/reduce_sum | solution.py:165
  149.7 8.7 %bitcast_add_fusion.2 = f32[1024,4,2,128]{0,3,2,1:T(8,128)} fusion(f32[1024,4,2,128]{0,3,2,1:T(8,128)} %get-tuple-element.276, f32[4,512,1024,2]{2,1,3,0:T(8,128)S(1)} %get-tuple-element.258, f32[1024,4,2]{0,2,1:T(2,128)S(1)} %fusion.138, pred[1024,512]{0,1:T(8,128)(4,1)S(1)} %compare_or_fusion.2, f32[1024,4,2]{0,2,1:T(2,128)S(1)} %get-tuple-element.260, ...), kind=kOutput, calls=%fused_computation.8.clone.1 | convolution fusion | flops 1097859072 | bytes 26279936 | tf_op jit(solution)/shard_map/while/body/eval_jaxpr/nkgp,pkd->nkgd/dot_general | solution.py:166
  158.4 5.4 %copy.208 = f32[1024,1024]{1,0:T(8,128)} copy(f32[1024,1024]{0,1:T(8,128)} %bitcast.172) | data formatting | bytes 8388608 | tf_op jit(solution)/shard_map/reshape;reshape | solution.py:187
  163.8 59.5 %pmax.7 = bf16[1024,8]{0,1:T(8,128)(2,1)S(1)} all-reduce(bf16[1024,8]{0,1:T(8,128)(2,1)S(1)} %convert_element_type.109), channel_id=1, replica_groups=mesh['kv'=2,'seq'=16] {'seq'}, use_global_device_ids=true, to_apply=%region_13.14 | all-reduce | flops 8192 | bytes 32768 | tf_op jit(solution)/shard_map/pmax | solution.py:185
  223.3 0.9 copy.213
  224.7 1.1 mul.385
  225.8 1.0 copy-done.1
  226.9 2.2 fusion.23
  229.1 0.7 rsqrt.35
  229.8 0.7 copy.220
  230.5 0.7 reshape.346
  231.2 0.7 rsqrt.36
  232.1 1.4 copy.176
  233.5 0.8 mul.436
  234.2 0.7 mul.437
  234.9 1.4 copy.191
  236.3 2.1 convolution_convert_fusion.2
  239.1 0.9 mul.399.clone
  240.0 0.7 mul.430
  240.7 0.8 fusion.47
  241.9 0.7 mul.441
  242.6 0.8 multiply_cosine_fusion
  243.5 1.4 fusion.102
  245.6 1.1 convolution_bitcast_fusion
  247.1 0.8 fusion.43
  248.0 0.7 compare_bitcast_fusion
  248.7 0.7 broadcast_bitcast_fusion.1
  249.4 0.9 fusion.82
  250.3 1.1 add_convert_fusion.1
  251.4 25.6 %reduce-scatter.10.cloned.1.call-done = bf16[64,8]{1,0:T(8,128)(2,1)} async-done(((bf16[1024,8]{1,0:T(8,128)(2,1)}), bf16[64,8]{1,0:T(8,128)(2,1)}) %reduce-scatter.10.cloned.1.call-update) | async-done | bytes 1040
  277.0 0.8 copy.214
  278.1 63.2 %reduce-scatter.6.cloned.1.call-done = bf16[64,1024]{1,0:T(8,128)(2,1)} async-done(((bf16[1024,1024]{1,0:T(8,128)(2,1)}), bf16[64,1024]{1,0:T(8,128)(2,1)}) %reduce-scatter.6.cloned.1.call-update) | async-done | bytes 131088 | tf_op jit(solution)/shard_map/reduce_scatter | solution.py:191
  341.3 0.9 mul.425
  342.6 3.9 %convolution_convert_fusion = bf16[64,2048]{1,0:T(8,128)(2,1)} fusion(bf16[1024,2048]{1,0:T(8,128)(2,1)} %param.24, f32[8,8,8,128]{3,2,1,0:T(8,128)S(1)} %bitcast.180, f32[8,8,8,128]{3,2,1,0:T(8,128)S(1)} %bitcast.183, f32[64,1024]{1,0:T(8,128)S(1)} %reshape.350, f32[8,8,8,128]{3,2,1,0:T(8,128)S(1)} %bitcast.181, f32[8,8,8,128]{3,2,1,0:T(8,128)S(1)} %bitcast.182, ...), kind=kOutput, calls=%fused_computation.37 | convolution fusion | flops 269025280 | bytes 5898240 | tf_op jit(solution)/shard_map/dot_general | solution.py:213
  346.8 0.7 fusion.100
  347.5 9.8 %reduce-scatter.8.cloned.1.call-done = bf16[64,1024]{1,0:T(8,128)(2,1)} async-done(((bf16[64,2048]{1,0:T(8,128)(2,1)}), bf16[64,1024]{1,0:T(8,128)(2,1)}) %reduce-scatter.8.cloned.1.call-update) | async-done | bytes 131088 | tf_op jit(solution)/shard_map/reduce_scatter | solution.py:214
  357.3 1.6 add_convert_fusion
  (175 shorter events, 12.3 us)
Async XLA Ops:
  7.2 17.1 %copy-start = (bf16[2048,512]{1,0:T(8,128)(2,1)S(1)}, bf16[2048,512]{1,0:T(8,128)(2,1)}, u32[]{:S(2)}) copy-start(bf16[2048,512]{1,0:T(8,128)(2,1)} %param.21) | copy-start | bytes 6291460
  7.2 11.9 %copy-start.21 = (f32[128]{0:T(128)S(1)}, f32[128]{0:T(128)}, u32[]{:S(2)}) copy-start(f32[128]{0:T(128)} %param.25) | copy-start | bytes 1540
  7.2 12.1 %copy-start.28 = (s32[2,32]{1,0:T(2,128)S(1)}, s32[2,32]{1,0:T(2,128)}, u32[]{:S(2)}) copy-start(s32[2,32]{1,0:T(2,128)} %param.32) | copy-start | bytes 772
  7.2 13.1 %copy-start.27 = (s32[32]{0:T(128)S(1)}, s32[32]{0:T(128)}, u32[]{:S(2)}) copy-start(s32[32]{0:T(128)} %param.30) | copy-start | bytes 388
  7.2 13.1 %copy-start.26 = (s32[32]{0:T(128)S(1)}, s32[32]{0:T(128)}, u32[]{:S(2)}) copy-start(s32[32]{0:T(128)} %param.31) | copy-start | bytes 388
  7.2 13.3 %copy-start.29 = (s32[4]{0:T(128)S(1)}, s32[4]{0:T(128)}, u32[]{:S(2)}) copy-start(s32[4]{0:T(128)} %param.29) | copy-start | bytes 52
  7.2 59.4 %all-gather.2.cloned.1.call-start = ((), (), s32[]{:S(2)}) async-start(), calls=%async_computation.3 | async-start | bytes 2228224 | tf_op jit(solution)/shard_map/all_gather | solution.py:140
  7.3 14.6 %copy-start.25 = (f32[64]{0:T(128)}, f32[64]{0:T(128)S(1)}, u32[]{:S(2)}) copy-start(f32[64]{0:T(128)S(1)} %multiply_exponential_fusion) | copy-start | bytes 772
  15.5 10.3 %copy-start.3 = (bf16[64,2048]{1,0:T(8,128)(2,1)}, bf16[64,2048]{1,0:T(8,128)(2,1)S(1)}, u32[]{:S(2)}) copy-start(bf16[64,2048]{1,0:T(8,128)(2,1)S(1)} %all_gather.6) | copy-start | bytes 786436
  15.6 10.2 %copy-start.22 = (f32[64]{0:T(128)}, f32[64]{0:T(128)S(1)}, u32[]{:S(2)}) copy-start(f32[64]{0:T(128)S(1)} %add_rsqrt_fusion.2) | copy-start | bytes 772
  15.6 8.6 %copy-start.19 = (f32[2048]{0:T(1024)S(1)}, f32[2048]{0:T(1024)}, u32[]{:S(2)}) copy-start(f32[2048]{0:T(1024)} %param.19) | copy-start | bytes 24580
  18.8 7.1 %copy-start.30 = (bf16[2048,8]{0,1:T(8,128)(2,1)S(1)}, bf16[2048,8]{0,1:T(8,128)(2,1)}, u32[]{:S(2)}) copy-start(bf16[2048,8]{0,1:T(8,128)(2,1)} %param.23) | copy-start | bytes 98308
  20.3 50.7 %copy-start.15 = (f32[2,32,32]{2,1,0:T(8,128)}, f32[2,32,32]{2,1,0:T(8,128)S(1)}, u32[]{:S(2)}) copy-start(f32[2,32,32]{2,1,0:T(8,128)S(1)} %get-tuple-element.190) | copy-start | bytes 24580
  21.3 49.8 %copy-start.24 = (f32[2,32]{1,0:T(2,128)}, f32[2,32]{1,0:T(2,128)S(1)}, u32[]{:S(2)}) copy-start(f32[2,32]{1,0:T(2,128)S(1)} %get-tuple-element.186) | copy-start | bytes 772
  21.7 0.8 copy-start.16
  21.7 0.6 copy-start.14
  21.9 0.7 copy-start.7
  21.9 0.8 copy-start.9
  23.6 253.4 %reduce-scatter.10.cloned.1.call-start = ((), (), s32[]{:S(2)}) async-start(), calls=%async_computation.6 | async-start | bytes 278528
  24.8 49.5 %copy-start.5 = (f32[64,512]{1,0:T(8,128)}, f32[64,512]{1,0:T(8,128)S(1)}, u32[]{:S(2)}) copy-start(f32[64,512]{1,0:T(8,128)S(1)} %fusion.94) | copy-start | bytes 393220
  82.8 4.2 %copy-start.2 = (bf16[1,512,4,128]{1,3,2,0:T(8,128)(2,1)S(1)}, bf16[1,512,4,128]{1,3,2,0:T(8,128)(2,1)}, u32[]{:S(2)}) copy-start(bf16[1,512,4,128]{1,3,2,0:T(8,128)(2,1)} %copy.285) | copy-start | bytes 1572868 | tf_op jit(solution)/shard_map/while
  102.7 4.2 %copy-start.2 = (bf16[1,512,4,128]{1,3,2,0:T(8,128)(2,1)S(1)}, bf16[1,512,4,128]{1,3,2,0:T(8,128)(2,1)}, u32[]{:S(2)}) copy-start(bf16[1,512,4,128]{1,3,2,0:T(8,128)(2,1)} %copy.285) | copy-start | bytes 1572868 | tf_op jit(solution)/shard_map/while
  124.1 4.2 %copy-start.2 = (bf16[1,512,4,128]{1,3,2,0:T(8,128)(2,1)S(1)}, bf16[1,512,4,128]{1,3,2,0:T(8,128)(2,1)}, u32[]{:S(2)}) copy-start(bf16[1,512,4,128]{1,3,2,0:T(8,128)(2,1)} %copy.285) | copy-start | bytes 1572868 | tf_op jit(solution)/shard_map/while
  145.5 4.2 %copy-start.2 = (bf16[1,512,4,128]{1,3,2,0:T(8,128)(2,1)S(1)}, bf16[1,512,4,128]{1,3,2,0:T(8,128)(2,1)}, u32[]{:S(2)}) copy-start(bf16[1,512,4,128]{1,3,2,0:T(8,128)(2,1)} %copy.285) | copy-start | bytes 1572868 | tf_op jit(solution)/shard_map/while
  224.2 117.1 %reduce-scatter.6.cloned.1.call-start = ((), (), s32[]{:S(2)}) async-start(), calls=%async_computation.4 | async-start | bytes 2228224 | tf_op jit(solution)/shard_map/reduce_scatter | solution.py:191
  224.7 2.2 copy-start.1
  226.9 3.6 copy-start.6
  226.9 9.5 %copy-start.4 = (bf16[64,2048]{1,0:T(8,128)(2,1)S(1)}, bf16[64,2048]{1,0:T(8,128)(2,1)}, u32[]{:S(2)}) copy-start(bf16[64,2048]{1,0:T(8,128)(2,1)} %copy-done.3) | copy-start | bytes 786436
  229.0 14.5 %copy-start.8 = (f32[64,8,64]{2,0,1:T(8,128)S(1)}, f32[64,8,64]{2,0,1:T(8,128)}, u32[]{:S(2)}) copy-start(f32[64,8,64]{2,0,1:T(8,128)} %copy-done.7) | copy-start | bytes 393220
  229.0 14.5 %copy-start.10 = (f32[64,8,64]{2,0,1:T(8,128)S(1)}, f32[64,8,64]{2,0,1:T(8,128)}, u32[]{:S(2)}) copy-start(f32[64,8,64]{2,0,1:T(8,128)} %copy-done.9) | copy-start | bytes 393220
  229.0 128.3 %reduce-scatter.8.cloned.1.call-start = ((), (), s32[]{:S(2)}) async-start(), calls=%async_computation.5 | async-start | bytes 393216 | tf_op jit(solution)/shard_map/reduce_scatter | solution.py:214
  229.1 2.1 copy-start.20
  232.1 9.6 %copy-start.17 = (f32[64,128]{1,0:T(8,128)S(1)}, f32[64,128]{1,0:T(8,128)}, u32[]{:S(2)}) copy-start(f32[64,128]{1,0:T(8,128)} %copy-done.16) | copy-start | bytes 98308
  238.5 1.6 copy-start.11
  244.9 0.6 copy-start.18
  247.1 99.4 %copy-start.12 = (bf16[64,512]{1,0:T(8,128)(2,1)S(1)}, bf16[64,512]{1,0:T(8,128)(2,1)}, u32[]{:S(2)}) copy-start(bf16[64,512]{1,0:T(8,128)(2,1)} %copy-done.11) | copy-start | bytes 196612
  247.1 99.4 %copy-start.23 = (f32[2,32]{1,0:T(2,128)S(1)}, f32[2,32]{1,0:T(2,128)}, u32[]{:S(2)}) copy-start(f32[2,32]{1,0:T(2,128)} %get-tuple-element.185) | copy-start | bytes 772
  251.4 105.9 %copy-start.13 = (bf16[64,1024]{1,0:T(8,128)(2,1)S(1)}, bf16[64,1024]{1,0:T(8,128)(2,1)}, u32[]{:S(2)}) copy-start(bf16[64,1024]{1,0:T(8,128)(2,1)} %param.18) | copy-start | bytes 393220
Sparse Core Ops, SparseCore 0:
  23.7 42.8 all-gather.1
  224.3 52.5 reduce-scatter.9
  280.7 60.5 reduce-scatter.5
  346.6 10.6 reduce-scatter.7
where the time goes:
time: 367 us; the launch traced here: 365 us
  waiting for transfers between devices  139 us (38%)
  blocking collectives  66.8 us (18%)
  matrix products  66.7 us (18%)
  local copies, waits for them, and re-layouts  47.5 us (13%)
  other arithmetic  30.8 us (8%)
  between operations  14.5 us (4%)
    reduce_scatter x1, waiting for transfers between devices, body(): lax.psum_scatter(scaled_num.astype(jnp.bfloat16), 'seq', scatter_dimensio...  63.2 us
    pmax x1, blocking collectives, body(): lax.pmax(part_max.astype(jnp.bfloat16), 'seq').astype(part_max.dtype)  59.5 us
    all_gather x1, waiting for transfers between devices, body(): query_piece = lax.all_gather(query_flat, 'seq', axis=0, tiled=True)  39.9 us
    dot_general x4, matrix products, visit(): jnp.einsum('nkgp,pkd->nkgd', weights.astype(jnp.bfloat16), values_block,...  33.2 us
    unnamed x5, waiting for transfers between devices  25.6 us
    dot_general x4, matrix products, visit(): jnp.einsum('nkgd,pkd->nkgp', grouped, keys_block, preferred_element_type=...  18.3 us
    reduce_sum x4, other arithmetic, visit(): run_sum = run_sum * factor + jnp.sum(weights, axis=-1)  16.3 us
    dynamic_slice x12, local copies, waits for them, and re-layouts, body(): lax.scan(visit, start_state, (key_blocks, value_blocks, segment_blocks))  14 us
  transfers between devices with their start and end apart: 4, of which 4 were waited for; matrix products, arithmetic and copies ran while one was open for 8% of the time, Pallas kernels for 0%

commit v1 on v0

--- a/solution.py
+++ b/solution.py
@@ -7,6 +7,19 @@
 EPSILON = 1e-06
 ROPE_BASE = 1000000.0
 NEGATIVE = -1e30
+
+
+def plan_rates(load, axis_name):
+    line_up = [load]
+    fan = lax.axis_size(axis_name)
+    for j in range(fan - 1):
+        opened = lax.ppermute(
+            line_up[-1], axis_name=axis_name, perm=[(s, (s + 1) % fan) for s in range(fan)]
+        )
+        line_up.append(opened)
+    later = jnp.concatenate(line_up[::-1], 0)
+    seen_now = lax.axis_index(axis_name)
+    return jnp.roll(later, (seen_now + 1) * load.shape[0], 0)
 
 
 def rms_scale(values, scales):
@@ -137,7 +150,7 @@
     value_blocks = pooled_cache_values.reshape(block_count, block_len, local_kv, head_width)
     segment_blocks = slot_segment.reshape(block_count, block_len)
     query_flat = query.reshape(local_tok, local_heads * head_width)
-    query_piece = lax.all_gather(query_flat, "seq", axis=0, tiled=True)
+    query_piece = plan_rates(query_flat, "seq")
     row_ids = jnp.arange(query_piece.shape[0], dtype=jnp.int32)
     owners = row_ids // tree
     count = query_piece.shape[0]

time: 367 us -> 430 us (1.17)
  waiting for transfers between devices: 139 us -> 215 us
  local copies, waits for them, and re-layouts: 47.5 us -> 39.2 us
    ppermute x0 -> x15, waiting for transfers between devices: none -> 99.2 us  [plan_rates(): lax.ppermute(line_up[-1], axis_name=axis_name, perm=[(s, (s + 1) % fan) f...]
    all_gather x1 -> x0, waiting for transfers between devices: 39.9 us -> none  [body(): query_piece = lax.all_gather(query_flat, 'seq', axis=0, tiled=True)]
    unnamed x5 -> x4, waiting for transfers between devices: 25.6 us -> 42.3 us
    reshape x1 -> x0, local copies, waits for them, and re-layouts: 4.48 us -> none  [body(): grouped = query_piece.reshape(count, local_kv, per_kv, head_width)]
    unnamed x66 -> x117, local copies, waits for them, and re-layouts: 8.05 us -> 11.2 us
  transfers between devices with their start and end apart: 4 -> 18, of which waited for: 4 -> 18; matrix products, arithmetic and copies ran while one was open for 8% -> 4% of each run, Pallas kernels for 0% -> 0%
where the time goes in v1:
time: 430 us; the launch traced here: 429 us
  waiting for transfers between devices  215 us (50%)
  matrix products  65.2 us (15%)
  blocking collectives  65 us (15%)
  local copies, waits for them, and re-layouts  39.2 us (9%)
  other arithmetic  29.2 us (7%)
  between operations  14.9 us (3%)
    ppermute x15, waiting for transfers between devices, plan_rates(): lax.ppermute(line_up[-1], axis_name=axis_name, perm=[(s, (s + 1) % fan) f...  99.2 us
    reduce_scatter x1, waiting for transfers between devices, body(): lax.psum_scatter(scaled_num.astype(jnp.bfloat16), 'seq', scatter_dimensio...  63.3 us
    pmax x1, blocking collectives, body(): lax.pmax(part_max.astype(jnp.bfloat16), 'seq').astype(part_max.dtype)  57.6 us
    unnamed x4, waiting for transfers between devices  42.3 us
    dot_general x4, matrix products, visit(): jnp.einsum('nkgp,pkd->nkgd', weights.astype(jnp.bfloat16), values_block,...  33.3 us
    dot_general x4, matrix products, visit(): jnp.einsum('nkgd,pkd->nkgp', grouped, keys_block, preferred_element_type=...  17.3 us
    reduce_sum x4, other arithmetic, visit(): run_sum = run_sum * factor + jnp.sum(weights, axis=-1)  16.3 us
    dynamic_slice x12, local copies, waits for them, and re-layouts, body(): lax.scan(visit, start_state, (key_blocks, value_blocks, segment_blocks))  14 us
  transfers between devices with their start and end apart: 18, of which 18 were waited for; matrix products, arithmetic and copies ran while one was open for 4% of the time, Pallas kernels for 0%

profile of v1, /device:TPU:0, one launch (start us, length us, event | category | flops | bytes accessed | tf_op | source)
XLA Modules:
  0.0 428.8 jit_solution(6113868158757689058)
XLA Ops:
  7.3 0.8 broadcast_bitcast_fusion
  8.1 7.4 %all_gather.3 = bf16[64,2048]{1,0:T(8,128)(2,1)S(1)} all-gather(bf16[64,1024]{1,0:T(8,128)(2,1)} %param.18), channel_id=1, replica_groups=mesh['kv'=2,'seq'=16] {'kv'}, dimensions={1}, use_global_device_ids=true | all-gather | bytes 393216 | tf_op jit(solution)/shard_map/all_gather | solution.py:97
  15.7 3.1 fusion.96
  20.1 0.8 fusion.101
  23.1 7.1 %collective-permute-done = bf16[64,1024]{1,0:T(8,128)(2,1)S(1)} collective-permute-done((bf16[64,1024]{1,0:T(8,128)(2,1)S(1)}, bf16[64,1024]{1,0:T(8,128)(2,1)S(1)}, u32[]{:S(2)}, u32[]{:S(2)}) %collective-permute-start) | collective-permute-done | bytes 131104 | tf_op jit(solution)/shard_map/ppermute | solution.py:16
  30.2 7.1 %collective-permute-done.1 = bf16[64,1024]{1,0:T(8,128)(2,1)S(1)} collective-permute-done((bf16[64,1024]{1,0:T(8,128)(2,1)S(1)}, bf16[64,1024]{1,0:T(8,128)(2,1)S(1)}, u32[]{:S(2)}, u32[]{:S(2)}) %collective-permute-start.1) | collective-permute-done | bytes 131104 | tf_op jit(solution)/shard_map/ppermute | solution.py:16
  37.3 7.1 %collective-permute-done.2 = bf16[64,1024]{1,0:T(8,128)(2,1)S(1)} collective-permute-done((bf16[64,1024]{1,0:T(8,128)(2,1)S(1)}, bf16[64,1024]{1,0:T(8,128)(2,1)S(1)}, u32[]{:S(2)}, u32[]{:S(2)}) %collective-permute-start.2) | collective-permute-done | bytes 131104 | tf_op jit(solution)/shard_map/ppermute | solution.py:16
  44.4 7.1 %collective-permute-done.3 = bf16[64,1024]{1,0:T(8,128)(2,1)S(1)} collective-permute-done((bf16[64,1024]{1,0:T(8,128)(2,1)S(1)}, bf16[64,1024]{1,0:T(8,128)(2,1)S(1)}, u32[]{:S(2)}, u32[]{:S(2)}) %collective-permute-start.3) | collective-permute-done | bytes 131104 | tf_op jit(solution)/shard_map/ppermute | solution.py:16
  51.5 7.1 %collective-permute-done.4 = bf16[64,1024]{1,0:T(8,128)(2,1)S(1)} collective-permute-done((bf16[64,1024]{1,0:T(8,128)(2,1)S(1)}, bf16[64,1024]{1,0:T(8,128)(2,1)S(1)}, u32[]{:S(2)}, u32[]{:S(2)}) %collective-permute-start.4) | collective-permute-done | bytes 131104 | tf_op jit(solution)/shard_map/ppermute | solution.py:16
  58.6 7.1 %collective-permute-done.5 = bf16[64,1024]{1,0:T(8,128)(2,1)S(1)} collective-permute-done((bf16[64,1024]{1,0:T(8,128)(2,1)S(1)}, bf16[64,1024]{1,0:T(8,128)(2,1)S(1)}, u32[]{:S(2)}, u32[]{:S(2)}) %collective-permute-start.5) | collective-permute-done | bytes 131104 | tf_op jit(solution)/shard_map/ppermute | solution.py:16
  65.7 7.1 %collective-permute-done.6 = bf16[64,1024]{1,0:T(8,128)(2,1)S(1)} collective-permute-done((bf16[64,1024]{1,0:T(8,128)(2,1)S(1)}, bf16[64,1024]{1,0:T(8,128)(2,1)S(1)}, u32[]{:S(2)}, u32[]{:S(2)}) %collective-permute-start.6) | collective-permute-done | bytes 131104 | tf_op jit(solution)/shard_map/ppermute | solution.py:16
  72.9 1.2 fusion.94
  74.1 0.8 fusion.91
  75.2 4.8 %collective-permute-done.7 = bf16[64,1024]{1,0:T(8,128)(2,1)} collective-permute-done((bf16[64,1024]{1,0:T(8,128)(2,1)S(1)}, bf16[64,1024]{1,0:T(8,128)(2,1)}, u32[]{:S(2)}, u32[]{:S(2)}) %collective-permute-start.7) | collective-permute-done | bytes 131104 | tf_op jit(solution)/shard_map/ppermute | solution.py:16
  80.0 1.6 fusion.28
  81.7 5.7 %collective-permute-done.8 = bf16[64,1024]{1,0:T(8,128)(2,1)S(1)} collective-permute-done((bf16[64,1024]{1,0:T(8,128)(2,1)}, bf16[64,1024]{1,0:T(8,128)(2,1)S(1)}, u32[]{:S(2)}, u32[]{:S(2)}) %collective-permute-start.8) | collective-permute-done | bytes 131104 | tf_op jit(solution)/shard_map/ppermute | solution.py:16
  87.3 1.4 broadcast_compare_fusion
  88.7 5.7 %collective-permute-done.9 = bf16[64,1024]{1,0:T(8,128)(2,1)S(1)} collective-permute-done((bf16[64,1024]{1,0:T(8,128)(2,1)S(1)}, bf16[64,1024]{1,0:T(8,128)(2,1)S(1)}, u32[]{:S(2)}, u32[]{:S(2)}) %collective-permute-start.9) | collective-permute-done | bytes 131104 | tf_op jit(solution)/shard_map/ppermute | solution.py:16
  95.2 6.3 %collective-permute-done.10 = bf16[64,1024]{1,0:T(8,128)(2,1)S(1)} collective-permute-done((bf16[64,1024]{1,0:T(8,128)(2,1)S(1)}, bf16[64,1024]{1,0:T(8,128)(2,1)S(1)}, u32[]{:S(2)}, u32[]{:S(2)}) %collective-permute-start.10) | collective-permute-done | bytes 131104 | tf_op jit(solution)/shard_map/ppermute | solution.py:16
  101.6 7.0 %collective-permute-done.11 = bf16[64,1024]{1,0:T(8,128)(2,1)S(1)} collective-permute-done((bf16[64,1024]{1,0:T(8,128)(2,1)S(1)}, bf16[64,1024]{1,0:T(8,128)(2,1)S(1)}, u32[]{:S(2)}, u32[]{:S(2)}) %collective-permute-start.11) | collective-permute-done | bytes 131104 | tf_op jit(solution)/shard_map/ppermute | solution.py:16
  108.8 6.9 %collective-permute-done.12 = bf16[64,1024]{1,0:T(8,128)(2,1)S(1)} collective-permute-done((bf16[64,1024]{1,0:T(8,128)(2,1)S(1)}, bf16[64,1024]{1,0:T(8,128)(2,1)S(1)}, u32[]{:S(2)}, u32[]{:S(2)}) %collective-permute-start.12) | collective-permute-done | bytes 131104 | tf_op jit(solution)/shard_map/ppermute | solution.py:16
  116.6 6.2 %collective-permute-done.13 = bf16[64,1024]{1,0:T(8,128)(2,1)S(1)} collective-permute-done((bf16[64,1024]{1,0:T(8,128)(2,1)S(1)}, bf16[64,1024]{1,0:T(8,128)(2,1)S(1)}, u32[]{:S(2)}, u32[]{:S(2)}) %collective-permute-start.13) | collective-permute-done | bytes 131104 | tf_op jit(solution)/shard_map/ppermute | solution.py:16
  122.8 7.1 %collective-permute-done.14 = bf16[64,1024]{1,0:T(8,128)(2,1)S(1)} collective-permute-done((bf16[64,1024]{1,0:T(8,128)(2,1)S(1)}, bf16[64,1024]{1,0:T(8,128)(2,1)S(1)}, u32[]{:S(2)}, u32[]{:S(2)}) %collective-permute-start.14) | collective-permute-done | bytes 131104 | tf_op jit(solution)/shard_map/ppermute | solution.py:16
  130.0 0.9 constant_dynamic-update-slice_fusion.24
  130.9 0.9 constant_dynamic-update-slice_fusion.23
  131.8 0.9 constant_dynamic-update-slice_fusion.22
  132.8 0.9 constant_dynamic-update-slice_fusion.21
  133.9 0.9 constant_dynamic-update-slice_fusion.8
  135.2 2.6 copy.173
  137.8 3.0 copy.176
  140.8 83.2 %while.15 = (s32[]{:T(128)}, f32[1024,4,2]{0,2,1:T(2,128)S(1)}, f32[1024,4,2]{0,2,1:T(2,128)S(1)}, f32[1024,4,2,128]{0,3,2,1:T(8,128)}, s32[4,512]{1,0:T(4,128)S...) while((s32[]{:T(128)}, f32[1024,4,2]{0,2,1:T(2,128)S(1)}, ...), condition=%wide.region_12.13_spmd.clone, body=%wide.region_9.12_spmd.clone.sunk | while | flops 2206780416 | bytes 69748896 | solution.py:192
  141.3 2.4 constant_dynamic-slice_fusion.7
  143.6 1.1 copy.289
  144.8 4.3 %fusion.137 = (f32[1024,4,2]{0,2,1:T(2,128)S(1)}, f32[4,512,1024,2]{2,1,3,0:T(8,128)S(1)}) fusion(pred[1024,512]{0,1:T(8,128)(4,1)S(1)} %compare_or_fusion.2, bf16[1024,4,2,128]{3,0,2,1:T(8,128)(2,1)S(1)} %get-tuple-element.282, bf16[1,512,4,128]{3,2,1,0:T(4,128)(2,1)} %get-tuple-element.247), kind=kOutput, calls=%fused_computation.3.clone.1 | convolution fusion | flops 1086316544 | bytes 19955712 | tf_op jit(solution)/shard_map/while/body/eval_jaxpr/nkgd,pkd->nkgp/dot_general | solution.py:167
  149.2 4.1 fusion.139
  153.3 7.2 %bitcast_add_fusion.2 = f32[1024,4,2,128]{0,3,2,1:T(8,128)} fusion(f32[1024,4,2,128]{0,3,2,1:T(8,128)} %get-tuple-element.267, f32[4,512,1024,2]{2,1,3,0:T(8,128)S(1)} %get-tuple-element.249, f32[1024,4,2]{0,2,1:T(2,128)S(1)} %fusion.138, pred[1024,512]{0,1:T(8,128)(4,1)S(1)} %compare_or_fusion.2, f32[1024,4,2]{0,2,1:T(2,128)S(1)} %get-tuple-element.251, ...), kind=kOutput, calls=%fused_computation.8.clone.1 | convolution fusion | flops 1097859072 | bytes 26279936 | tf_op jit(solution)/shard_map/while/body/eval_jaxpr/nkgp,pkd->nkgd/dot_general | solution.py:179
  160.9 2.4 constant_dynamic-slice_fusion.7
  163.3 1.1 copy.289
  164.4 4.3 %fusion.137 = (f32[1024,4,2]{0,2,1:T(2,128)S(1)}, f32[4,512,1024,2]{2,1,3,0:T(8,128)S(1)}) fusion(pred[1024,512]{0,1:T(8,128)(4,1)S(1)} %compare_or_fusion.2, bf16[1024,4,2,128]{3,0,2,1:T(8,128)(2,1)S(1)} %get-tuple-element.282, bf16[1,512,4,128]{3,2,1,0:T(4,128)(2,1)} %get-tuple-element.247), kind=kOutput, calls=%fused_computation.3.clone.1 | convolution fusion | flops 1086316544 | bytes 19955712 | tf_op jit(solution)/shard_map/while/body/eval_jaxpr/nkgd,pkd->nkgp/dot_general | solution.py:167
  168.8 4.1 fusion.139
  173.0 8.7 %bitcast_add_fusion.2 = f32[1024,4,2,128]{0,3,2,1:T(8,128)} fusion(f32[1024,4,2,128]{0,3,2,1:T(8,128)} %get-tuple-element.267, f32[4,512,1024,2]{2,1,3,0:T(8,128)S(1)} %get-tuple-element.249, f32[1024,4,2]{0,2,1:T(2,128)S(1)} %fusion.138, pred[1024,512]{0,1:T(8,128)(4,1)S(1)} %compare_or_fusion.2, f32[1024,4,2]{0,2,1:T(2,128)S(1)} %get-tuple-element.251, ...), kind=kOutput, calls=%fused_computation.8.clone.1 | convolution fusion | flops 1097859072 | bytes 26279936 | tf_op jit(solution)/shard_map/while/body/eval_jaxpr/nkgp,pkd->nkgd/dot_general | solution.py:179
  182.1 2.4 constant_dynamic-slice_fusion.7
  184.5 1.1 copy.289
  185.6 4.3 %fusion.137 = (f32[1024,4,2]{0,2,1:T(2,128)S(1)}, f32[4,512,1024,2]{2,1,3,0:T(8,128)S(1)}) fusion(pred[1024,512]{0,1:T(8,128)(4,1)S(1)} %compare_or_fusion.2, bf16[1024,4,2,128]{3,0,2,1:T(8,128)(2,1)S(1)} %get-tuple-element.282, bf16[1,512,4,128]{3,2,1,0:T(4,128)(2,1)} %get-tuple-element.247), kind=kOutput, calls=%fused_computation.3.clone.1 | convolution fusion | flops 1086316544 | bytes 19955712 | tf_op jit(solution)/shard_map/while/body/eval_jaxpr/nkgd,pkd->nkgp/dot_general | solution.py:167
  190.0 4.1 fusion.139
  194.1 8.7 %bitcast_add_fusion.2 = f32[1024,4,2,128]{0,3,2,1:T(8,128)} fusion(f32[1024,4,2,128]{0,3,2,1:T(8,128)} %get-tuple-element.267, f32[4,512,1024,2]{2,1,3,0:T(8,128)S(1)} %get-tuple-element.249, f32[1024,4,2]{0,2,1:T(2,128)S(1)} %fusion.138, pred[1024,512]{0,1:T(8,128)(4,1)S(1)} %compare_or_fusion.2, f32[1024,4,2]{0,2,1:T(2,128)S(1)} %get-tuple-element.251, ...), kind=kOutput, calls=%fused_computation.8.clone.1 | convolution fusion | flops 1097859072 | bytes 26279936 | tf_op jit(solution)/shard_map/while/body/eval_jaxpr/nkgp,pkd->nkgd/dot_general | solution.py:179
  203.3 2.4 constant_dynamic-slice_fusion.7
  205.7 1.1 copy.289
  206.8 4.3 %fusion.137 = (f32[1024,4,2]{0,2,1:T(2,128)S(1)}, f32[4,512,1024,2]{2,1,3,0:T(8,128)S(1)}) fusion(pred[1024,512]{0,1:T(8,128)(4,1)S(1)} %compare_or_fusion.2, bf16[1024,4,2,128]{3,0,2,1:T(8,128)(2,1)S(1)} %get-tuple-element.282, bf16[1,512,4,128]{3,2,1,0:T(4,128)(2,1)} %get-tuple-element.247), kind=kOutput, calls=%fused_computation.3.clone.1 | convolution fusion | flops 1086316544 | bytes 19955712 | tf_op jit(solution)/shard_map/while/body/eval_jaxpr/nkgd,pkd->nkgp/dot_general | solution.py:167
  211.2 4.1 fusion.139
  215.3 8.7 %bitcast_add_fusion.2 = f32[1024,4,2,128]{0,3,2,1:T(8,128)} fusion(f32[1024,4,2,128]{0,3,2,1:T(8,128)} %get-tuple-element.267, f32[4,512,1024,2]{2,1,3,0:T(8,128)S(1)} %get-tuple-element.249, f32[1024,4,2]{0,2,1:T(2,128)S(1)} %fusion.138, pred[1024,512]{0,1:T(8,128)(4,1)S(1)} %compare_or_fusion.2, f32[1024,4,2]{0,2,1:T(2,128)S(1)} %get-tuple-element.251, ...), kind=kOutput, calls=%fused_computation.8.clone.1 | convolution fusion | flops 1097859072 | bytes 26279936 | tf_op jit(solution)/shard_map/while/body/eval_jaxpr/nkgp,pkd->nkgd/dot_general | solution.py:179
  224.0 5.4 %copy.212 = f32[1024,1024]{1,0:T(8,128)} copy(f32[1024,1024]{0,1:T(8,128)} %bitcast.174) | data formatting | bytes 8388608 | tf_op jit(solution)/shard_map/reshape;reshape | solution.py:200
  229.5 57.6 %pmax.7 = bf16[1024,8]{0,1:T(8,128)(2,1)S(1)} all-reduce(bf16[1024,8]{0,1:T(8,128)(2,1)S(1)} %convert_element_type.109), channel_id=1, replica_groups=mesh['kv'=2,'seq'=16] {'seq'}, use_global_device_ids=true, to_apply=%region_13.14 | all-reduce | flops 8192 | bytes 32768 | tf_op jit(solution)/shard_map/pmax | solution.py:198
  287.2 0.8 copy.217
  288.3 1.1 mul.389
  289.5 1.0 copy-done.2
  290.6 2.2 fusion.23
  293.9 2.1 convolution_convert_fusion.2
  298.8 42.2 %reduce-scatter.10.cloned.1.call-done = bf16[64,8]{1,0:T(8,128)(2,1)} async-done(((bf16[1024,8]{1,0:T(8,128)(2,1)}), bf16[64,8]{1,0:T(8,128)(2,1)}) %reduce-scatter.10.cloned.1.call-update) | async-done | bytes 1040
  341.0 0.8 copy.218
  342.1 63.3 %reduce-scatter.6.cloned.1.call-done = bf16[64,1024]{1,0:T(8,128)(2,1)} async-done(((bf16[1024,1024]{1,0:T(8,128)(2,1)}), bf16[64,1024]{1,0:T(8,128)(2,1)}) %reduce-scatter.6.cloned.1.call-update) | async-done | bytes 131088 | tf_op jit(solution)/shard_map/reduce_scatter | solution.py:204
  405.9 3.9 convolution_convert_fusion
  410.9 9.8 %reduce-scatter.8.cloned.1.call-done = bf16[64,1024]{1,0:T(8,128)(2,1)} async-done(((bf16[64,2048]{1,0:T(8,128)(2,1)}), bf16[64,1024]{1,0:T(8,128)(2,1)}) %reduce-scatter.8.cloned.1.call-update) | async-done | bytes 131088 | tf_op jit(solution)/shard_map/reduce_scatter | solution.py:227
  420.7 1.6 add_convert_fusion
  (255 shorter events, 14.3 us)
Async XLA Ops:
  7.2 65.7 %copy-start = (bf16[2048,512]{1,0:T(8,128)(2,1)S(1)}, bf16[2048,512]{1,0:T(8,128)(2,1)}, u32[]{:S(2)}) copy-start(bf16[2048,512]{1,0:T(8,128)(2,1)} %param.21) | copy-start | bytes 6291460
  7.2 12.0 %copy-start.26 = (f32[128]{0:T(128)S(1)}, f32[128]{0:T(128)}, u32[]{:S(2)}) copy-start(f32[128]{0:T(128)} %param.25) | copy-start | bytes 1540
  7.2 12.1 %copy-start.38 = (s32[2,32]{1,0:T(2,128)S(1)}, s32[2,32]{1,0:T(2,128)}, u32[]{:S(2)}) copy-start(s32[2,32]{1,0:T(2,128)} %param.32) | copy-start | bytes 772
  7.2 13.6 %copy-start.37 = (s32[32]{0:T(128)S(1)}, s32[32]{0:T(128)}, u32[]{:S(2)}) copy-start(s32[32]{0:T(128)} %param.30) | copy-start | bytes 388
  7.2 13.6 %copy-start.36 = (s32[32]{0:T(128)S(1)}, s32[32]{0:T(128)}, u32[]{:S(2)}) copy-start(s32[32]{0:T(128)} %param.31) | copy-start | bytes 388
  7.2 13.8 %copy-start.39 = (s32[4]{0:T(128)S(1)}, s32[4]{0:T(128)}, u32[]{:S(2)}) copy-start(s32[4]{0:T(128)} %param.29) | copy-start | bytes 52
  7.2 333.8 %reduce-scatter.10.cloned.1.call-start = ((), (), s32[]{:S(2)}) async-start(), calls=%async_computation.5 | async-start | bytes 278528
  7.3 15.1 %copy-start.34 = (f32[64]{0:T(128)}, f32[64]{0:T(128)S(1)}, u32[]{:S(2)}) copy-start(f32[64]{0:T(128)S(1)} %multiply_exponential_fusion) | copy-start | bytes 772
  15.5 64.6 %copy-start.4 = (bf16[64,2048]{1,0:T(8,128)(2,1)}, bf16[64,2048]{1,0:T(8,128)(2,1)S(1)}, u32[]{:S(2)}) copy-start(bf16[64,2048]{1,0:T(8,128)(2,1)S(1)} %all_gather.3) | copy-start | bytes 786436
  15.6 3.3 copy-start.28
  15.6 57.2 %copy-start.24 = (f32[2048]{0:T(1024)S(1)}, f32[2048]{0:T(1024)}, u32[]{:S(2)}) copy-start(f32[2048]{0:T(1024)} %param.19) | copy-start | bytes 24580
  21.8 1.1 copy-start.31
  22.2 50.7 %copy-start.22 = (f32[64,128]{1,0:T(8,128)}, f32[64,128]{1,0:T(8,128)S(1)}, u32[]{:S(2)}) copy-start(f32[64,128]{1,0:T(8,128)S(1)} %pad_maximum_fusion.1) | copy-start | bytes 98308
  22.3 0.6 copy-start.19
  22.4 50.3 %copy-start.8 = (f32[64,8,64]{2,0,1:T(8,128)}, f32[64,8,64]{2,0,1:T(8,128)S(1)}, u32[]{:S(2)}) copy-start(f32[64,8,64]{2,0,1:T(8,128)S(1)} %get-tuple-element.168) | copy-start | bytes 393220
  22.4 50.4 %copy-start.10 = (f32[64,8,64]{2,0,1:T(8,128)}, f32[64,8,64]{2,0,1:T(8,128)S(1)}, u32[]{:S(2)}) copy-start(f32[64,8,64]{2,0,1:T(8,128)S(1)} %get-tuple-element.169) | copy-start | bytes 393220
  23.1 7.1 %collective-permute-start = (bf16[64,1024]{1,0:T(8,128)(2,1)S(1)}, bf16[64,1024]{1,0:T(8,128)(2,1)S(1)}, u32[]{:S(2)}, u32[]{:S(2)}) collective-permute-start(bf16[64,1024]{1,0:T(8,128)(2,1)S(1)} %fusion.35), channel_id=1, source_target_pairs={{0,1},{1,2},{2,3},{3,4},{4,5},{5,6},{6,7},{7,8},{8,9},{9,10},{10,1... | collective-permute-start | bytes 393224 | tf_op jit(solution)/shard_map/ppermute | solution.py:16
  30.2 7.1 %collective-permute-start.1 = (bf16[64,1024]{1,0:T(8,128)(2,1)S(1)}, bf16[64,1024]{1,0:T(8,128)(2,1)S(1)}, u32[]{:S(2)}, u32[]{:S(2)}) collective-permute-start(bf16[64,1024]{1,0:T(8,128)(2,1)S(1)} %collective-permute-done), channel_id=1, source_target_pairs={{0,1},{1,2},{2,3},{3,4},{4,5},{5,6},{6,7},{7,8},{8,9},{9,10},{10,1... | collective-permute-start | bytes 393224 | tf_op jit(solution)/shard_map/ppermute | solution.py:16
  37.3 7.1 %collective-permute-start.2 = (bf16[64,1024]{1,0:T(8,128)(2,1)S(1)}, bf16[64,1024]{1,0:T(8,128)(2,1)S(1)}, u32[]{:S(2)}, u32[]{:S(2)}) collective-permute-start(bf16[64,1024]{1,0:T(8,128)(2,1)S(1)} %collective-permute-done.1), channel_id=1, source_target_pairs={{0,1},{1,2},{2,3},{3,4},{4,5},{5,6},{6,7},{7,8},{8,9},{9,10},{10,1... | collective-permute-start | bytes 393224 | tf_op jit(solution)/shard_map/ppermute | solution.py:16
  44.4 7.1 %collective-permute-start.3 = (bf16[64,1024]{1,0:T(8,128)(2,1)S(1)}, bf16[64,1024]{1,0:T(8,128)(2,1)S(1)}, u32[]{:S(2)}, u32[]{:S(2)}) collective-permute-start(bf16[64,1024]{1,0:T(8,128)(2,1)S(1)} %collective-permute-done.2), channel_id=1, source_target_pairs={{0,1},{1,2},{2,3},{3,4},{4,5},{5,6},{6,7},{7,8},{8,9},{9,10},{10,1... | collective-permute-start | bytes 393224 | tf_op jit(solution)/shard_map/ppermute | solution.py:16
  51.5 7.1 %collective-permute-start.4 = (bf16[64,1024]{1,0:T(8,128)(2,1)S(1)}, bf16[64,1024]{1,0:T(8,128)(2,1)S(1)}, u32[]{:S(2)}, u32[]{:S(2)}) collective-permute-start(bf16[64,1024]{1,0:T(8,128)(2,1)S(1)} %collective-permute-done.3), channel_id=1, source_target_pairs={{0,1},{1,2},{2,3},{3,4},{4,5},{5,6},{6,7},{7,8},{8,9},{9,10},{10,1... | collective-permute-start | bytes 393224 | tf_op jit(solution)/shard_map/ppermute | solution.py:16
  58.6 14.2 %copy-start.13 = (bf16[64,1024]{1,0:T(8,128)(2,1)}, bf16[64,1024]{1,0:T(8,128)(2,1)S(1)}, u32[]{:S(2)}) copy-start(bf16[64,1024]{1,0:T(8,128)(2,1)S(1)} %collective-permute-done.4) | copy-start | bytes 393220
  58.6 7.1 %collective-permute-start.5 = (bf16[64,1024]{1,0:T(8,128)(2,1)S(1)}, bf16[64,1024]{1,0:T(8,128)(2,1)S(1)}, u32[]{:S(2)}, u32[]{:S(2)}) collective-permute-start(bf16[64,1024]{1,0:T(8,128)(2,1)S(1)} %collective-permute-done.4), channel_id=1, source_target_pairs={{0,1},{1,2},{2,3},{3,4},{4,5},{5,6},{6,7},{7,8},{8,9},{9,10},{10,1... | collective-permute-start | bytes 393224 | tf_op jit(solution)/shard_map/ppermute | solution.py:16
  65.7 7.1 %copy-start.15 = (bf16[64,1024]{1,0:T(8,128)(2,1)}, bf16[64,1024]{1,0:T(8,128)(2,1)S(1)}, u32[]{:S(2)}) copy-start(bf16[64,1024]{1,0:T(8,128)(2,1)S(1)} %collective-permute-done.5) | copy-start | bytes 393220
  65.7 7.1 %collective-permute-start.6 = (bf16[64,1024]{1,0:T(8,128)(2,1)S(1)}, bf16[64,1024]{1,0:T(8,128)(2,1)S(1)}, u32[]{:S(2)}, u32[]{:S(2)}) collective-permute-start(bf16[64,1024]{1,0:T(8,128)(2,1)S(1)} %collective-permute-done.5), channel_id=1, source_target_pairs={{0,1},{1,2},{2,3},{3,4},{4,5},{5,6},{6,7},{7,8},{8,9},{9,10},{10,1... | collective-permute-start | bytes 393224 | tf_op jit(solution)/shard_map/ppermute | solution.py:16
  72.8 42.9 %copy-start.17 = (bf16[64,1024]{1,0:T(8,128)(2,1)}, bf16[64,1024]{1,0:T(8,128)(2,1)S(1)}, u32[]{:S(2)}) copy-start(bf16[64,1024]{1,0:T(8,128)(2,1)S(1)} %collective-permute-done.6) | copy-start | bytes 393220
  72.8 7.2 %collective-permute-start.7 = (bf16[64,1024]{1,0:T(8,128)(2,1)S(1)}, bf16[64,1024]{1,0:T(8,128)(2,1)}, u32[]{:S(2)}, u32[]{:S(2)}) collective-permute-start(bf16[64,1024]{1,0:T(8,128)(2,1)S(1)} %collective-permute-done.6), channel_id=1, source_target_pairs={{0,1},{1,2},{2,3},{3,4},{4,5},{5,6},{6,7},{7,8},{8,9},{9,10},{10,1... | collective-permute-start | bytes 393224 | tf_op jit(solution)/shard_map/ppermute | solution.py:16
  74.1 60.8 %copy-start.6 = (f32[64,512]{1,0:T(8,128)}, f32[64,512]{1,0:T(8,128)S(1)}, u32[]{:S(2)}) copy-start(f32[64,512]{1,0:T(8,128)S(1)} %fusion.94) | copy-start | bytes 393220
  74.1 60.7 %copy-start.16 = (bf16[64,1024]{1,0:T(8,128)(2,1)S(1)}, bf16[64,1024]{1,0:T(8,128)(2,1)}, u32[]{:S(2)}) copy-start(bf16[64,1024]{1,0:T(8,128)(2,1)} %copy-done.15) | copy-start | bytes 393220
  74.1 60.8 %copy-start.14 = (bf16[64,1024]{1,0:T(8,128)(2,1)S(1)}, bf16[64,1024]{1,0:T(8,128)(2,1)}, u32[]{:S(2)}) copy-start(bf16[64,1024]{1,0:T(8,128)(2,1)} %copy-done.13) | copy-start | bytes 393220
  80.0 7.3 %collective-permute-start.8 = (bf16[64,1024]{1,0:T(8,128)(2,1)}, bf16[64,1024]{1,0:T(8,128)(2,1)S(1)}, u32[]{:S(2)}, u32[]{:S(2)}) collective-permute-start(bf16[64,1024]{1,0:T(8,128)(2,1)} %collective-permute-done.7), channel_id=1, source_target_pairs={{0,1},{1,2},{2,3},{3,4},{4,5},{5,6},{6,7},{7,8},{8,9},{9,10},{10,1... | collective-permute-start | bytes 393224 | tf_op jit(solution)/shard_map/ppermute | solution.py:16
  87.3 7.1 %collective-permute-start.9 = (bf16[64,1024]{1,0:T(8,128)(2,1)S(1)}, bf16[64,1024]{1,0:T(8,128)(2,1)S(1)}, u32[]{:S(2)}, u32[]{:S(2)}) collective-permute-start(bf16[64,1024]{1,0:T(8,128)(2,1)S(1)} %collective-permute-done.8), channel_id=1, source_target_pairs={{0,1},{1,2},{2,3},{3,4},{4,5},{5,6},{6,7},{7,8},{8,9},{9,10},{10,1... | collective-permute-start | bytes 393224 | tf_op jit(solution)/shard_map/ppermute | solution.py:16
  94.4 7.1 %collective-permute-start.10 = (bf16[64,1024]{1,0:T(8,128)(2,1)S(1)}, bf16[64,1024]{1,0:T(8,128)(2,1)S(1)}, u32[]{:S(2)}, u32[]{:S(2)}) collective-permute-start(bf16[64,1024]{1,0:T(8,128)(2,1)S(1)} %collective-permute-done.9), channel_id=1, source_target_pairs={{0,1},{1,2},{2,3},{3,4},{4,5},{5,6},{6,7},{7,8},{8,9},{9,10},{10,1... | collective-permute-start | bytes 393224 | tf_op jit(solution)/shard_map/ppermute | solution.py:16
  101.5 7.1 %collective-permute-start.11 = (bf16[64,1024]{1,0:T(8,128)(2,1)S(1)}, bf16[64,1024]{1,0:T(8,128)(2,1)S(1)}, u32[]{:S(2)}, u32[]{:S(2)}) collective-permute-start(bf16[64,1024]{1,0:T(8,128)(2,1)S(1)} %collective-permute-done.10), channel_id=1, source_target_pairs={{0,1},{1,2},{2,3},{3,4},{4,5},{5,6},{6,7},{7,8},{8,9},{9,10},{10,1... | collective-permute-start | bytes 393224 | tf_op jit(solution)/shard_map/ppermute | solution.py:16
  108.6 7.1 %collective-permute-start.12 = (bf16[64,1024]{1,0:T(8,128)(2,1)S(1)}, bf16[64,1024]{1,0:T(8,128)(2,1)S(1)}, u32[]{:S(2)}, u32[]{:S(2)}) collective-permute-start(bf16[64,1024]{1,0:T(8,128)(2,1)S(1)} %collective-permute-done.11), channel_id=1, source_target_pairs={{0,1},{1,2},{2,3},{3,4},{4,5},{5,6},{6,7},{7,8},{8,9},{9,10},{10,1... | collective-permute-start | bytes 393224 | tf_op jit(solution)/shard_map/ppermute | solution.py:16
  115.7 7.1 %collective-permute-start.13 = (bf16[64,1024]{1,0:T(8,128)(2,1)S(1)}, bf16[64,1024]{1,0:T(8,128)(2,1)S(1)}, u32[]{:S(2)}, u32[]{:S(2)}) collective-permute-start(bf16[64,1024]{1,0:T(8,128)(2,1)S(1)} %collective-permute-done.12), channel_id=1, source_target_pairs={{0,1},{1,2},{2,3},{3,4},{4,5},{5,6},{6,7},{7,8},{8,9},{9,10},{10,1... | collective-permute-start | bytes 393224 | tf_op jit(solution)/shard_map/ppermute | solution.py:16
  115.7 19.1 %copy-start.18 = (bf16[64,1024]{1,0:T(8,128)(2,1)S(1)}, bf16[64,1024]{1,0:T(8,128)(2,1)}, u32[]{:S(2)}) copy-start(bf16[64,1024]{1,0:T(8,128)(2,1)} %copy-done.17) | copy-start | bytes 393220
  122.8 7.1 %collective-permute-start.14 = (bf16[64,1024]{1,0:T(8,128)(2,1)S(1)}, bf16[64,1024]{1,0:T(8,128)(2,1)S(1)}, u32[]{:S(2)}, u32[]{:S(2)}) collective-permute-start(bf16[64,1024]{1,0:T(8,128)(2,1)S(1)} %collective-permute-done.13), channel_id=1, source_target_pairs={{0,1},{1,2},{2,3},{3,4},{4,5},{5,6},{6,7},{7,8},{8,9},{9,10},{10,1... | collective-permute-start | bytes 393224 | tf_op jit(solution)/shard_map/ppermute | solution.py:16
  149.1 4.2 copy-start.3
  168.8 4.2 copy-start.3
  190.0 4.2 copy-start.3
  211.2 4.2 copy-start.3
  288.1 117.3 %reduce-scatter.6.cloned.1.call-start = ((), (), s32[]{:S(2)}) async-start(), calls=%async_computation.3 | async-start | bytes 2228224 | tf_op jit(solution)/shard_map/reduce_scatter | solution.py:204
  288.3 2.2 copy-start.2
  290.5 2.7 copy-start.7
  290.5 3.1 copy-start.25
  290.5 3.2 copy-start.20
  290.5 3.3 copy-start.33
  290.5 3.4 copy-start.5
  290.5 3.4 copy-start.29
  292.7 3.6 copy-start.27
  292.7 3.8 copy-start.23
  292.7 4.1 copy-start.32
  292.7 4.1 copy-start.35
  292.7 4.4 %copy-start.9 = (f32[64,8,64]{2,0,1:T(8,128)S(1)}, f32[64,8,64]{2,0,1:T(8,128)}, u32[]{:S(2)}) copy-start(f32[64,8,64]{2,0,1:T(8,128)} %copy-done.8) | copy-start | bytes 393220
  292.7 4.4 %copy-start.11 = (f32[64,8,64]{2,0,1:T(8,128)S(1)}, f32[64,8,64]{2,0,1:T(8,128)}, u32[]{:S(2)}) copy-start(f32[64,8,64]{2,0,1:T(8,128)} %copy-done.10) | copy-start | bytes 393220
  292.8 127.9 %reduce-scatter.8.cloned.1.call-start = ((), (), s32[]{:S(2)}) async-start(), calls=%async_computation.4 | async-start | bytes 393216 | tf_op jit(solution)/shard_map/reduce_scatter | solution.py:227
  293.9 4.6 %copy-start.40 = (s32[2]{0:T(128)S(1)}, s32[2]{0:T(128)}, u32[]{:S(2)}) copy-start(s32[2]{0:T(128)} %param.33) | copy-start | bytes 28
  293.9 4.7 %copy-start.21 = (f32[2,32,32]{2,1,0:T(8,128)S(1)}, f32[2,32,32]{2,1,0:T(8,128)}, u32[]{:S(2)}) copy-start(f32[2,32,32]{2,1,0:T(8,128)} %get-tuple-element.181) | copy-start | bytes 24580
  298.3 111.6 %copy-start.30 = (f32[2,32]{1,0:T(2,128)S(1)}, f32[2,32]{1,0:T(2,128)}, u32[]{:S(2)}) copy-start(f32[2,32]{1,0:T(2,128)} %get-tuple-element.176) | copy-start | bytes 772
  298.8 121.9 %copy-start.12 = (bf16[64,1024]{1,0:T(8,128)(2,1)S(1)}, bf16[64,1024]{1,0:T(8,128)(2,1)}, u32[]{:S(2)}) copy-start(bf16[64,1024]{1,0:T(8,128)(2,1)} %param.18) | copy-start | bytes 393220
  341.9 80.4 %copy-start.1 = (bf16[2048,512]{1,0:T(8,128)(2,1)S(1)}, bf16[2048,512]{1,0:T(8,128)(2,1)}, u32[]{:S(2)}) copy-start(bf16[2048,512]{1,0:T(8,128)(2,1)} %param.21) | copy-start | bytes 6291460
Sparse Core Ops, SparseCore 0:
  288.2 52.7 reduce-scatter.9
  344.8 60.6 reduce-scatter.5
  410.0 10.6 reduce-scatter.7
